TPU v7x, 256 devices: a whole 4x4x8 slice. The times are simulated.
256 devices in a mesh: cuts: 4 (over y), blk: 64 (over x, z, core).
Axes of the slice: x: 4, y: 4, z: 8, core: 2. Of those that a mesh axis runs over, the one named last changes fastest.
Arguments:
- gap_load: float32 [4, 128, 2, 256, 128], P('cuts', 'blk'), may hold values from -24 to 24
- offsets: int32 [4, 128, 2], P('cuts', 'blk'), may hold values from -1 to 255, as said below
- corner_map: int32 [4, 128, 4], P('cuts', 'blk'), may hold values from -1 to 511, as said below
- flexibility: float32 [4, 128, 1024, 1024], P('cuts', 'blk'), may hold values from -0.5 to 4.5, as said below
- coupling: float32 [4, 128, 12, 1024], P('cuts', 'blk'), may hold values from -1.25 to 1.25
- corner_rows: float32 [4, 128, 12, 1536], P('cuts', 'blk'), may hold values from -0.1 to 1.1, as said below
Outputs:
- multipliers: float32 [4, 128, 2, 256, 128], P('cuts', 'blk')
- residual: float32 [4, 128, 2, 256, 128], P('cuts', 'blk')
Inputs may be any that keep to these rules, and one draw needn't show every extreme that they name: `offsets`: on an interface owned by a subdomain, the neighbour's dof k matches the owner's dof (k + offset) mod 256; -1 marks an interface without multipliers: the tunnel's far end, or one that touches an excavated subdomain. `corner_map`: entries k = 0, 1, 2, 3 are the corners at near-left, near-right, far-left, far-right. Entry 2 of subdomain (r, c) is never -1, and every node is entry 2 of exactly one subdomain; the same node is entry 3 of (r, (c - 1) mod 128) and, for r + 1 < 4, entries 0 of (r + 1, c) and 1 of (r + 1, (c - 1) mod 128), and no other entry. -1 marks a clamped corner at the tunnel's near end. `flexibility`: each block is symmetric positive definite. `corner_rows`: row 3 k + j of a subdomain is row 3 m + j of one symmetric positive definite matrix of order 3 * 512, with m = corner_map entry k; zero rows where that entry is -1.
All inputs are finite; a program needn't handle non-finite values.
Results may differ from a plain program's by a relative error of at most 0.00021.
Values sent between devices are 32-bit elements; how exact they have to be, the bound alone decides.
A program may use at most 64 MiB of HBM per device.

v0:
```python
import jax
import jax.numpy as jnp
from jax import lax
from jax.sharding import PartitionSpec as P

ITERS = 3
HIGH = lax.Precision.HIGHEST


def from_behind(value, axis, steps):
    count = lax.axis_size(axis)
    first, last = (max(0, -steps), min(count, count - steps))
    return lax.ppermute(value, axis, [(source, source + steps) for source in range(first, last)])


def passed_along(value, axis, steps):
    count = lax.axis_size(axis)
    pairs = [(source, (source + steps) % count) for source in range(count)]
    return lax.ppermute(value, axis, pairs)


def rotate(values, amounts, orient):
    face_size = values.shape[-2]
    indices = (jnp.arange(face_size, dtype=jnp.int32) + orient * amounts[..., None]) % face_size
    return jnp.take_along_axis(values, indices[..., None], axis=-2)


def corner_indices(corner_map, dof_count):
    spread = 3 * corner_map[..., None] + jnp.arange(3, dtype=jnp.int32)
    spread = jnp.where(corner_map[..., None] >= 0, spread, dof_count)
    return spread.reshape(corner_map.shape[0], corner_map.shape[1], 12)


def inner_sum(first, second):
    return jnp.sum(first * second, axis=(0, 1, 2, 3))


def squares(residual):
    return lax.psum(inner_sum(residual, residual), ("cuts", "blk"))


def per_device(gap_load, offsets, corner_map, flexibility, coupling, corner_rows):
    cycle_count, circ_count, _, face_size, load_count = gap_load.shape
    dof_count = corner_rows.shape[-1]
    active = (offsets >= 0).astype(jnp.float32)[..., None, None]
    corner_dofs = corner_indices(corner_map, dof_count)
    residual = gap_load * active
    multipliers = jnp.zeros_like(residual)
    direction = residual
    norm_now = squares(residual)
    for iteration in range(ITERS):
        sent_far = -rotate(direction[:, :, 0], offsets[:, :, 0], 1)
        sent_right = -rotate(direction[:, :, 1], offsets[:, :, 1], 1)
        edge_near = from_behind(sent_far[-1], "cuts", 1)
        edge_left = passed_along(sent_right[:, -1], "blk", 1)
        nearside = jnp.concatenate([edge_near[None], sent_far[:-1]], axis=0)
        leftside = jnp.concatenate([edge_left[:, None], sent_right[:, :-1]], axis=1)
        loads = jnp.stack([nearside, direction[:, :, 0], leftside, direction[:, :, 1]], axis=2)
        loads = loads.reshape(cycle_count, circ_count, 4 * face_size, load_count)
        operator_corner_terms = jnp.einsum("rcki,rcin->rckn", coupling, loads, precision=HIGH)
        partial_value = jnp.zeros((dof_count, load_count), jnp.float32)
        partial_value = partial_value.at[corner_dofs.reshape(-1)].add(
            operator_corner_terms.reshape(-1, load_count), mode="drop"
        )
        coarse = lax.psum(partial_value, ("cuts", "blk"))
        corner_values = jnp.einsum("rckm,mn->rckn", corner_rows, coarse, precision=HIGH)
        moved = jnp.einsum("rcij,rcjn->rcin", flexibility, loads, precision=HIGH)
        moved = moved + jnp.einsum("rcki,rckn->rcin", coupling, corner_values, precision=HIGH)
        moved = moved.reshape(cycle_count, circ_count, 4, face_size, load_count)
        from_far = from_behind(moved[0, :, 0], "cuts", -1)
        from_right = passed_along(moved[:, 0, 2], "blk", -1)
        far_near = jnp.concatenate([moved[1:, :, 0], from_far[None]], axis=0)
        right_left = jnp.concatenate([moved[:, 1:, 2], from_right[:, None]], axis=1)
        jump_far = moved[:, :, 1] - rotate(far_near, offsets[:, :, 0], -1)
        jump_right = moved[:, :, 3] - rotate(right_left, offsets[:, :, 1], -1)
        mapped = jnp.stack([jump_far, jump_right], axis=2) * active
        step_size = norm_now / lax.psum(inner_sum(direction, mapped), ("cuts", "blk"))
        multipliers = multipliers + step_size * direction
        residual = residual - step_size * mapped
        norm_next = squares(residual)
        direction = residual + norm_next / norm_now * direction
        norm_now = norm_next
    return (multipliers, residual)


def solution(mesh):
    in_specs = (
        P("cuts", "blk", None, None, None),
        P("cuts", "blk", None),
        P("cuts", "blk", None),
        P("cuts", "blk", None, None),
        P("cuts", "blk", None, None),
        P("cuts", "blk", None, None),
    )
    out_specs = (P("cuts", "blk", None, None, None), P("cuts", "blk", None, None, None))
    return jax.shard_map(
        per_device, mesh=mesh, in_specs=in_specs, out_specs=out_specs, check_vma=False
    )
```

profile of v0, /device:TPU:1, one launch (start us, length us, event | category | flops | bytes accessed | tf_op | source)
XLA Modules:
  0.0 1306.6 jit_solution(7525697432891195552)
XLA Ops:
  10.4 3.7 gather_fusion.1
  14.3 3.1 collective-permute-start.1
  17.6 3.7 gather_fusion
  21.4 3.2 collective-permute-start
  25.0 4.6 collective-permute-done
  33.4 11.0 fusion.4
  44.4 248.0 %all-reduce.5.cloned.1.call-done = f32[1536,128]{1,0:T(8,128)} async-done(((f32[1536,128]{1,0:T(8,128)}), f32[1536,128]{1,0:T(8,128)}) %all-reduce.5.cloned.1.call-update) | async-done | bytes 786448 | tf_op jit(solution)/shard_map/psum | solution.py:65
  298.3 2.4 collective-permute-start.3
  303.1 3.7 gather_fusion.3
  308.9 3.7 gather_fusion.2
  312.9 78.9 %all-reduce = (f32[128]{0:T(128)S(1)}, f32[128]{0:T(128)S(1)}) all-reduce(f32[128]{0:T(128)S(1)} %get-tuple-element.8, f32[128]{0:T(128)S(1)} %get-tuple-element.7), channel_id=1, replica_groups=mesh['cuts'=4,'blk'=64] {'cuts','blk'}, use_global_device_ids=true, to_apply=%region_1.2 | all-reduce | flops 256 | bytes 2048 | tf_op jit(solution)/shard_map/psum | solution.py:39
  392.0 72.6 %psum.66 = f32[128]{0:T(128)S(1)} all-reduce(f32[128]{0:T(128)S(1)} %multiply_reduce_fusion.3), channel_id=1, replica_groups=mesh['cuts'=4,'blk'=64] {'cuts','blk'}, use_global_device_ids=true, to_apply=%region_7.9 | all-reduce | flops 128 | bytes 1024 | tf_op jit(solution)/shard_map/psum | solution.py:39
  464.9 3.7 gather_fusion.4
  468.7 3.7 gather_fusion.5
  472.5 2.4 collective-permute-start.4
  475.0 2.7 collective-permute-start.5
  483.9 11.0 fusion.2
  494.9 243.5 %all-reduce.7.cloned.1.call-done = f32[1536,128]{1,0:T(8,128)} async-done(((f32[1536,128]{1,0:T(8,128)}), f32[1536,128]{1,0:T(8,128)}) %all-reduce.7.cloned.1.call-update) | async-done | bytes 786448 | tf_op jit(solution)/shard_map/psum | solution.py:65
  750.5 3.7 gather_fusion.7
  755.2 3.7 gather_fusion.6
  759.9 80.2 %psum.68 = f32[128]{0:T(128)S(1)} all-reduce(f32[128]{0:T(128)S(1)} %multiply_reduce_fusion.2), channel_id=1, replica_groups=mesh['cuts'=4,'blk'=64] {'cuts','blk'}, use_global_device_ids=true, to_apply=%region_11.13 | all-reduce | flops 128 | bytes 1024 | tf_op jit(solution)/shard_map/psum | solution.py:77
  840.9 72.8 %psum.69 = f32[128]{0:T(128)S(1)} all-reduce(f32[128]{0:T(128)S(1)} %get-tuple-element.15), channel_id=1, replica_groups=mesh['cuts'=4,'blk'=64] {'cuts','blk'}, use_global_device_ids=true, to_apply=%region_13.15 | all-reduce | flops 128 | bytes 1024 | tf_op jit(solution)/shard_map/psum | solution.py:39
  915.3 3.7 gather_fusion.8
  919.8 3.7 gather_fusion.9
  925.8 2.7 collective-permute-start.9
  936.7 12.0 fusion
  948.8 242.0 %all-reduce.9.cloned.1.call-done = f32[1536,128]{1,0:T(8,128)} async-done(((f32[1536,128]{1,0:T(8,128)}), f32[1536,128]{1,0:T(8,128)}) %all-reduce.9.cloned.1.call-update) | async-done | bytes 786448 | tf_op jit(solution)/shard_map/psum | solution.py:65
  1192.5 3.3 fusion.6
  1200.1 2.3 collective-permute-start.11
  1210.8 3.7 gather_fusion.11
  1215.9 3.7 gather_fusion.10
  1220.0 77.9 %psum.71 = f32[128]{0:T(128)S(1)} all-reduce(f32[128]{0:T(128)S(1)} %multiply_reduce_fusion), channel_id=1, replica_groups=mesh['cuts'=4,'blk'=64] {'cuts','blk'}, use_global_device_ids=true, to_apply=%region_17.19 | all-reduce | flops 128 | bytes 1024 | tf_op jit(solution)/shard_map/psum | solution.py:77
  (161 shorter events, 71.3 us)
Async XLA Ops:
  7.2 285.2 %copy-start = (f32[1,2,12,1536]{3,1,2,0:T(2,128)S(1)}, f32[1,2,12,1536]{3,1,2,0:T(2,128)}, u32[]{:S(2)}) copy-start(f32[1,2,12,1536]{3,1,2,0:T(2,128)} %param.13) | copy-start | bytes 442372
  7.2 17.4 %copy-start.12 = (s32[1,2,4]{2,1,0:T(2,128)S(1)}, s32[1,2,4]{2,1,0:T(2,128)}, u32[]{:S(2)}) copy-start(s32[1,2,4]{2,1,0:T(2,128)} %param.10) | copy-start | bytes 100
  7.2 23.5 %copy-start.2 = (f32[1,2,12,1024]{3,1,2,0:T(2,128)S(1)}, f32[1,2,12,1024]{3,1,2,0:T(2,128)}, u32[]{:S(2)}) copy-start(f32[1,2,12,1024]{3,1,2,0:T(2,128)} %param.12) | copy-start | bytes 294916
  7.2 285.2 %all-reduce.5.cloned.1.call-start = ((), (), s32[]{:S(2)}) async-start(), calls=%async_computation | async-start | bytes 1572864 | tf_op jit(solution)/shard_map/psum | solution.py:65
  9.0 463.4 %copy-start.5 = (pred[2,256]{1,0:T(4,128)(4,1)}, pred[2,256]{1,0:T(4,128)(4,1)S(1)}, u32[]{:S(2)}) copy-start(pred[2,256]{1,0:T(4,128)(4,1)S(1)} %and_bitcast_fusion.2) | copy-start | bytes 1540
  14.3 10.7 collective-permute-start.1
  17.5 451.1 %copy-start.7 = (pred[2,256]{1,0:T(4,128)(4,1)}, pred[2,256]{1,0:T(4,128)(4,1)S(1)}, u32[]{:S(2)}) copy-start(pred[2,256]{1,0:T(4,128)(4,1)S(1)} %and_bitcast_fusion.3) | copy-start | bytes 1540
  21.4 8.3 collective-permute-start
  25.0 457.0 %copy-start.13 = (s32[24]{0:T(128)}, s32[24]{0:T(128)S(1)}, u32[]{:S(2)}) copy-start(s32[24]{0:T(128)S(1)} %fusion.45) | copy-start | bytes 292
  33.3 705.1 %all-reduce.7.cloned.1.call-start = ((), (), s32[]{:S(2)}) async-start(), calls=%async_computation.1 | async-start | bytes 1572864 | tf_op jit(solution)/shard_map/psum | solution.py:65
  292.4 20.3 %copy-start.1 = (f32[1,2,2,256,128]{4,3,2,1,0:T(8,128)S(1)}, f32[1,2,2,256,128]{4,3,2,1,0:T(8,128)}, u32[]{:S(2)}) copy-start(f32[1,2,2,256,128]{4,3,2,1,0:T(8,128)} %param.8) | copy-start | bytes 1572868
  298.3 4.8 collective-permute-start.3
  301.8 7.1 collective-permute-start.2
  464.6 16.3 %copy-start.14 = (f32[128]{0:T(128)}, f32[128]{0:T(128)S(1)}, u32[]{:S(2)}) copy-start(f32[128]{0:T(128)S(1)} %psum.66) | copy-start | bytes 1540
  464.6 16.3 %copy-start.8 = (f32[128]{0:T(128)}, f32[128]{0:T(128)S(1)}, u32[]{:S(2)}) copy-start(f32[128]{0:T(128)S(1)} %div.16) | copy-start | bytes 1540
  472.5 7.4 collective-permute-start.4
  475.0 4.6 collective-permute-start.5
  483.6 707.2 %all-reduce.9.cloned.1.call-start = ((), (), s32[]{:S(2)}) async-start(), calls=%async_computation.2 | async-start | bytes 1572864 | tf_op jit(solution)/shard_map/psum | solution.py:65
  744.9 4.7 collective-permute-start.7
  748.1 7.1 collective-permute-start.6
  755.2 168.2 %copy-start.6 = (pred[2,256]{1,0:T(4,128)(4,1)S(1)}, pred[2,256]{1,0:T(4,128)(4,1)}, u32[]{:S(2)}) copy-start(pred[2,256]{1,0:T(4,128)(4,1)} %copy-done.5) | copy-start | bytes 1540
  840.7 91.5 %copy-start.10 = (f32[128]{0:T(128)}, f32[128]{0:T(128)S(1)}, u32[]{:S(2)}) copy-start(f32[128]{0:T(128)S(1)} %div.17) | copy-start | bytes 1540
  840.9 73.4 %copy-start.3 = (f32[1,2,2,256,128]{4,3,1,2,0:T(8,128)}, f32[1,2,2,256,128]{4,3,1,2,0:T(8,128)S(1)}, u32[]{:S(2)}) copy-start(f32[1,2,2,256,128]{4,3,1,2,0:T(8,128)S(1)} %get-tuple-element.16) | copy-start | bytes 1572868
  913.7 20.2 %copy-start.15 = (f32[128]{0:T(128)}, f32[128]{0:T(128)S(1)}, u32[]{:S(2)}) copy-start(f32[128]{0:T(128)S(1)} %psum.69) | copy-start | bytes 1540
  923.6 7.2 collective-permute-start.8
  925.8 4.6 collective-permute-start.9
  1192.5 105.4 %copy-start.4 = (f32[1,2,2,256,128]{4,3,1,2,0:T(8,128)S(1)}, f32[1,2,2,256,128]{4,3,1,2,0:T(8,128)}, u32[]{:S(2)}) copy-start(f32[1,2,2,256,128]{4,3,1,2,0:T(8,128)} %copy-done.3) | copy-start | bytes 1572868
  1192.5 105.4 %copy-start.9 = (f32[128]{0:T(128)S(1)}, f32[128]{0:T(128)}, u32[]{:S(2)}) copy-start(f32[128]{0:T(128)} %copy-done.8) | copy-start | bytes 1540
  1192.5 105.4 %copy-start.11 = (f32[128]{0:T(128)S(1)}, f32[128]{0:T(128)}, u32[]{:S(2)}) copy-start(f32[128]{0:T(128)} %copy-done.10) | copy-start | bytes 1540
  1195.8 102.1 %copy-start.16 = (f32[128]{0:T(128)S(1)}, f32[128]{0:T(128)}, u32[]{:S(2)}) copy-start(f32[128]{0:T(128)} %copy-done.15) | copy-start | bytes 1540
  1200.1 9.8 collective-permute-start.11
  1208.6 7.3 collective-permute-start.10
Sparse Core Ops, SparseCore 0:
  33.4 258.9 all-reduce.4
  483.7 254.6 all-reduce.6
  936.8 253.8 all-reduce.8
where the time goes:
time: 1320 us; the launch traced here: 1310 us
  waiting for transfers between devices  746 us (57%)
  blocking collectives  382 us (29%)
  local copies, waits for them, and re-layouts  68.4 us (5%)
  matrix products  49.6 us (4%)
  starting transfers between devices  27.4 us (2%)
  other arithmetic  18.2 us (1%)
  between operations  14.7 us (1%)
    psum x3, waiting for transfers between devices, per_device(): coarse = lax.psum(partial_value, ('cuts', 'blk'))  733 us
    psum x3, blocking collectives, squares(): return lax.psum(inner_sum(residual, residual), ('cuts', 'blk'))  224 us
    psum x2, blocking collectives, per_device(): lax.psum(inner_sum(direction, mapped), ('cuts', 'blk'))  158 us
    gather x12, local copies, waits for them, and re-layouts, rotate(): return jnp.take_along_axis(values, indices[..., None], axis=-2)  43.9 us
    dot_general x3, matrix products, per_device(): moved = jnp.einsum('rcij,rcjn->rcin', flexibility, loads, precision=HIGH)  34.1 us
  transfers between devices with their start and end apart: 15, of which 12 were waited for; matrix products, arithmetic and copies ran while one was open for 5% of the time, Pallas kernels for 0%

commit v1 on v0

--- a/solution.py
+++ b/solution.py
@@ -74,7 +74,7 @@
         jump_far = moved[:, :, 1] - rotate(far_near, offsets[:, :, 0], -1)
         jump_right = moved[:, :, 3] - rotate(right_left, offsets[:, :, 1], -1)
         mapped = jnp.stack([jump_far, jump_right], axis=2) * active
-        step_size = norm_now / lax.psum(inner_sum(direction, mapped), ("cuts", "blk"))
+        step_size = norm_now / lax.psum(lax.psum(inner_sum(direction, mapped), "blk"), "cuts")
         multipliers = multipliers + step_size * direction
         residual = residual - step_size * mapped
         norm_next = squares(residual)

time: 1320 us -> 1570 us (1.19)
  blocking collectives: 382 us -> 636 us
    psum x2 -> x6, blocking collectives: 158 us -> 407 us  [the longest x3 384 us: per_device(): lax.psum(inner_sum(direction, mapped), 'blk')]
  transfers between devices with their start and end apart: 15 -> 15, of which waited for: 12 -> 12; matrix products, arithmetic and copies ran while one was open for 5% -> 4% of each run, Pallas kernels for 0% -> 0%
where the time goes in v1:
time: 1570 us; the launch traced here: 1560 us
  waiting for transfers between devices  744 us (47%)
  blocking collectives  636 us (41%)
  local copies, waits for them, and re-layouts  68.4 us (4%)
  matrix products  49.6 us (3%)
  starting transfers between devices  28.2 us (2%)
  other arithmetic  18.2 us (1%)
    psum x3, waiting for transfers between devices, per_device(): coarse = lax.psum(partial_value, ('cuts', 'blk'))  730 us
    psum x3, blocking collectives, per_device(): lax.psum(inner_sum(direction, mapped), 'blk')  384 us
    psum x3, blocking collectives, squares(): return lax.psum(inner_sum(residual, residual), ('cuts', 'blk'))  228 us
    gather x12, local copies, waits for them, and re-layouts, rotate(): return jnp.take_along_axis(values, indices[..., None], axis=-2)  43.9 us
    dot_general x3, matrix products, per_device(): moved = jnp.einsum('rcij,rcjn->rcin', flexibility, loads, precision=HIGH)  34.1 us
  transfers between devices with their start and end apart: 15, of which 12 were waited for; matrix products, arithmetic and copies ran while one was open for 4% of the time, Pallas kernels for 0%

profile of v1, /device:TPU:1, one launch (start us, length us, event | category | flops | bytes accessed | tf_op | source)
XLA Modules:
  0.0 1558.9 jit_solution(14081481286458546857)
XLA Ops:
  10.4 3.7 gather_fusion.1
  14.3 3.1 collective-permute-start.1
  17.6 3.7 gather_fusion
  21.4 3.2 collective-permute-start
  25.0 4.6 collective-permute-done
  33.4 11.0 fusion.4
  44.4 248.0 %all-reduce.4.cloned.1.call-done = f32[1536,128]{1,0:T(8,128)} async-done(((f32[1536,128]{1,0:T(8,128)}), f32[1536,128]{1,0:T(8,128)}) %all-reduce.4.cloned.1.call-update) | async-done | bytes 786448 | tf_op jit(solution)/shard_map/psum | solution.py:65
  303.1 3.7 gather_fusion.3
  308.9 3.7 gather_fusion.2
  312.9 128.0 %psum.86 = f32[128]{0:T(128)S(1)} all-reduce(f32[128]{0:T(128)S(1)} %get-tuple-element.7), channel_id=1, replica_groups=mesh['cuts'=4,'blk'=64] {'blk'}, use_global_device_ids=true, to_apply=%region_5.7 | all-reduce | flops 128 | bytes 1024 | tf_op jit(solution)/shard_map/psum | solution.py:77
  440.9 7.2 psum.87
  448.1 76.6 %psum.84 = f32[128]{0:T(128)S(1)} all-reduce(f32[128]{0:T(128)S(1)} %get-tuple-element.8), channel_id=1, replica_groups=mesh['cuts'=4,'blk'=64] {'cuts','blk'}, use_global_device_ids=true, to_apply=%region_1.2 | all-reduce | flops 128 | bytes 1024 | tf_op jit(solution)/shard_map/psum | solution.py:39
  524.8 74.4 %psum.88 = f32[128]{0:T(128)S(1)} all-reduce(f32[128]{0:T(128)S(1)} %multiply_reduce_fusion.3), channel_id=1, replica_groups=mesh['cuts'=4,'blk'=64] {'cuts','blk'}, use_global_device_ids=true, to_apply=%region_8.10 | all-reduce | flops 128 | bytes 1024 | tf_op jit(solution)/shard_map/psum | solution.py:39
  599.5 3.7 gather_fusion.4
  603.3 3.7 gather_fusion.5
  619.1 11.0 fusion.2
  630.1 241.5 %all-reduce.6.cloned.1.call-done = f32[1536,128]{1,0:T(8,128)} async-done(((f32[1536,128]{1,0:T(8,128)}), f32[1536,128]{1,0:T(8,128)}) %all-reduce.6.cloned.1.call-update) | async-done | bytes 786448 | tf_op jit(solution)/shard_map/psum | solution.py:65
  883.7 3.7 gather_fusion.7
  888.4 3.7 gather_fusion.6
  893.1 128.0 %psum.90 = f32[128]{0:T(128)S(1)} all-reduce(f32[128]{0:T(128)S(1)} %multiply_reduce_fusion.2), channel_id=1, replica_groups=mesh['cuts'=4,'blk'=64] {'blk'}, use_global_device_ids=true, to_apply=%region_12.14 | all-reduce | flops 128 | bytes 1024 | tf_op jit(solution)/shard_map/psum | solution.py:77
  1021.1 7.7 psum.91
  1029.7 77.5 %psum.92 = f32[128]{0:T(128)S(1)} all-reduce(f32[128]{0:T(128)S(1)} %get-tuple-element.13), channel_id=1, replica_groups=mesh['cuts'=4,'blk'=64] {'cuts','blk'}, use_global_device_ids=true, to_apply=%region_15.17 | all-reduce | flops 128 | bytes 1024 | tf_op jit(solution)/shard_map/psum | solution.py:39
  1108.8 3.7 gather_fusion.8
  1113.3 3.7 gather_fusion.9
  1117.1 3.2 collective-permute-start.8
  1131.2 12.0 fusion
  1143.2 240.9 %all-reduce.8.cloned.1.call-done = f32[1536,128]{1,0:T(8,128)} async-done(((f32[1536,128]{1,0:T(8,128)}), f32[1536,128]{1,0:T(8,128)}) %all-reduce.8.cloned.1.call-update) | async-done | bytes 786448 | tf_op jit(solution)/shard_map/psum | solution.py:65
  1385.9 3.3 fusion.6
  1404.4 3.7 gather_fusion.11
  1409.5 3.7 gather_fusion.10
  1413.5 128.0 %psum.94 = f32[128]{0:T(128)S(1)} all-reduce(f32[128]{0:T(128)S(1)} %multiply_reduce_fusion), channel_id=1, replica_groups=mesh['cuts'=4,'blk'=64] {'blk'}, use_global_device_ids=true, to_apply=%region_19.21 | all-reduce | flops 128 | bytes 1024 | tf_op jit(solution)/shard_map/psum | solution.py:77
  1541.4 8.4 psum.95
  (165 shorter events, 82.3 us)
Async XLA Ops:
  7.2 285.2 %copy-start = (f32[1,2,12,1536]{3,1,2,0:T(2,128)S(1)}, f32[1,2,12,1536]{3,1,2,0:T(2,128)}, u32[]{:S(2)}) copy-start(f32[1,2,12,1536]{3,1,2,0:T(2,128)} %param.13) | copy-start | bytes 442372
  7.2 17.4 %copy-start.12 = (s32[1,2,4]{2,1,0:T(2,128)S(1)}, s32[1,2,4]{2,1,0:T(2,128)}, u32[]{:S(2)}) copy-start(s32[1,2,4]{2,1,0:T(2,128)} %param.10) | copy-start | bytes 100
  7.2 23.5 %copy-start.2 = (f32[1,2,12,1024]{3,1,2,0:T(2,128)S(1)}, f32[1,2,12,1024]{3,1,2,0:T(2,128)}, u32[]{:S(2)}) copy-start(f32[1,2,12,1024]{3,1,2,0:T(2,128)} %param.12) | copy-start | bytes 294916
  7.2 285.2 %all-reduce.4.cloned.1.call-start = ((), (), s32[]{:S(2)}) async-start(), calls=%async_computation | async-start | bytes 1572864 | tf_op jit(solution)/shard_map/psum | solution.py:65
  9.0 598.0 %copy-start.5 = (pred[2,256]{1,0:T(4,128)(4,1)}, pred[2,256]{1,0:T(4,128)(4,1)S(1)}, u32[]{:S(2)}) copy-start(pred[2,256]{1,0:T(4,128)(4,1)S(1)} %and_bitcast_fusion.2) | copy-start | bytes 1540
  14.3 10.7 collective-permute-start.1
  17.5 585.7 %copy-start.7 = (pred[2,256]{1,0:T(4,128)(4,1)}, pred[2,256]{1,0:T(4,128)(4,1)S(1)}, u32[]{:S(2)}) copy-start(pred[2,256]{1,0:T(4,128)(4,1)S(1)} %and_bitcast_fusion.3) | copy-start | bytes 1540
  21.4 8.3 collective-permute-start
  25.0 592.2 %copy-start.13 = (s32[24]{0:T(128)}, s32[24]{0:T(128)S(1)}, u32[]{:S(2)}) copy-start(s32[24]{0:T(128)S(1)} %fusion.45) | copy-start | bytes 292
  33.3 838.3 %all-reduce.6.cloned.1.call-start = ((), (), s32[]{:S(2)}) async-start(), calls=%async_computation.1 | async-start | bytes 1572864 | tf_op jit(solution)/shard_map/psum | solution.py:65
  292.4 20.3 %copy-start.1 = (f32[1,2,2,256,128]{4,3,2,1,0:T(8,128)S(1)}, f32[1,2,2,256,128]{4,3,2,1,0:T(8,128)}, u32[]{:S(2)}) copy-start(f32[1,2,2,256,128]{4,3,2,1,0:T(8,128)} %param.8) | copy-start | bytes 1572868
  298.3 4.8 collective-permute-start.3
  301.7 7.1 collective-permute-start.2
  599.2 15.9 %copy-start.14 = (f32[128]{0:T(128)}, f32[128]{0:T(128)S(1)}, u32[]{:S(2)}) copy-start(f32[128]{0:T(128)S(1)} %psum.88) | copy-start | bytes 1540
  599.2 15.9 %copy-start.8 = (f32[128]{0:T(128)}, f32[128]{0:T(128)S(1)}, u32[]{:S(2)}) copy-start(f32[128]{0:T(128)S(1)} %div.16) | copy-start | bytes 1540
  607.1 8.0 collective-permute-start.4
  610.2 3.8 collective-permute-start.5
  618.8 765.4 %all-reduce.8.cloned.1.call-start = ((), (), s32[]{:S(2)}) async-start(), calls=%async_computation.2 | async-start | bytes 1572864 | tf_op jit(solution)/shard_map/psum | solution.py:65
  878.1 4.7 collective-permute-start.7
  881.3 7.1 collective-permute-start.6
  888.4 228.5 %copy-start.6 = (pred[2,256]{1,0:T(4,128)(4,1)S(1)}, pred[2,256]{1,0:T(4,128)(4,1)}, u32[]{:S(2)}) copy-start(pred[2,256]{1,0:T(4,128)(4,1)} %copy-done.5) | copy-start | bytes 1540
  1029.4 97.2 %copy-start.10 = (f32[128]{0:T(128)}, f32[128]{0:T(128)S(1)}, u32[]{:S(2)}) copy-start(f32[128]{0:T(128)S(1)} %div.17) | copy-start | bytes 1540
  1029.7 78.2 %copy-start.3 = (f32[1,2,2,256,128]{4,3,1,2,0:T(8,128)}, f32[1,2,2,256,128]{4,3,1,2,0:T(8,128)S(1)}, u32[]{:S(2)}) copy-start(f32[1,2,2,256,128]{4,3,1,2,0:T(8,128)S(1)} %get-tuple-element.14) | copy-start | bytes 1572868
  1107.2 21.2 %copy-start.15 = (f32[128]{0:T(128)}, f32[128]{0:T(128)S(1)}, u32[]{:S(2)}) copy-start(f32[128]{0:T(128)S(1)} %psum.92) | copy-start | bytes 1540
  1117.1 8.2 collective-permute-start.8
  1120.3 4.6 collective-permute-start.9
  1385.9 164.0 %copy-start.4 = (f32[1,2,2,256,128]{4,3,1,2,0:T(8,128)S(1)}, f32[1,2,2,256,128]{4,3,1,2,0:T(8,128)}, u32[]{:S(2)}) copy-start(f32[1,2,2,256,128]{4,3,1,2,0:T(8,128)} %copy-done.3) | copy-start | bytes 1572868
  1385.9 164.0 %copy-start.9 = (f32[128]{0:T(128)S(1)}, f32[128]{0:T(128)}, u32[]{:S(2)}) copy-start(f32[128]{0:T(128)} %copy-done.8) | copy-start | bytes 1540
  1385.9 164.0 %copy-start.11 = (f32[128]{0:T(128)S(1)}, f32[128]{0:T(128)}, u32[]{:S(2)}) copy-start(f32[128]{0:T(128)} %copy-done.10) | copy-start | bytes 1540
  1389.2 160.7 %copy-start.16 = (f32[128]{0:T(128)S(1)}, f32[128]{0:T(128)}, u32[]{:S(2)}) copy-start(f32[128]{0:T(128)} %copy-done.15) | copy-start | bytes 1540
  1393.5 9.9 collective-permute-start.11
  1402.1 7.3 collective-permute-start.10
Sparse Core Ops, SparseCore 0:
  33.4 258.9 all-reduce.3
  618.9 252.6 all-reduce.5
  1131.3 252.7 all-reduce.7
